TPU v7x, 512 devices: a whole 4x8x8 slice. The times are simulated.
512 devices in a mesh: mod: 2 (over z_hi), loop: 16 (over x, z_lo), line: 16 (over y, core).
Axes of the slice: x: 4, y: 8, z: 8 (z_hi: 2, z_lo: 4; z = z_hi * 4 + z_lo), core: 2. Of those that a mesh axis runs over, the one named last changes fastest.
Arguments:
- act: bfloat16 [2, 196608, 512], P('mod', ('loop', 'line'))
- dy: bfloat16 [2, 196608, 1280], P('mod', ('loop', 'line')), may hold values from -6 to 6
- w_out: bfloat16 [2, 512, 1280], P('mod'), may hold values from -0.15625 to 0.15625
- counts: int32 [2, 16, 16], P('mod', 'loop', 'line'), may hold values from 192 to 768, as said below
Outputs:
- grad_clipped: float32 [2, 512, 1280], P('mod', 'loop')
- hidden_grad: bfloat16 [2, 196608, 512], P('mod', ('loop', 'line'))
Inputs may be any that keep to these rules, and one draw needn't show every extreme that they name: `counts`: in each tower some device has all 768 slots live.
All inputs are finite; a program needn't handle non-finite values.
Results may differ from a plain program's by a relative error of at most 0.001.
Values sent between devices are 32-bit elements; how exact they have to be, the bound alone decides.
A program may use at most 64 MiB of HBM per device.

v0:
```python
import jax
import jax.numpy as jnp
from jax import lax
from jax.sharding import PartitionSpec as P


def on_device(act, dy, w_out, counts):
    tokens = act[0]
    upstream = dy[0]
    weight = w_out[0]
    rows = tokens.shape[0]
    hidden = tokens.shape[1]
    block = weight.shape[1]
    live = lax.broadcasted_iota(jnp.int32, (rows, 1), 0) < counts[0, 0]
    masked = jnp.where(live, tokens, jnp.zeros_like(tokens))
    entries = lax.axis_size("mod") * hidden * block
    share = lax.psum_scatter(
        lax.dot_general(
            masked, upstream, (((0,), (0,)), ((), ())), preferred_element_type=jnp.float32
        ),
        "loop",
        scatter_dimension=0,
        tiled=True,
    )
    share = lax.psum(share, "line")
    total = lax.psum(jnp.sum(share * share), ("mod", "loop"))
    factor = 1.0 / jnp.sqrt(total / entries + 1e-06)
    clipped = share * factor
    back = lax.dot_general(
        upstream, weight, (((1,), (1,)), ((), ())), preferred_element_type=jnp.float32
    )
    hidden_grad = jnp.where(live, back, jnp.zeros_like(back)).astype(jnp.bfloat16)
    return (clipped[None], hidden_grad[None])


def solution(mesh):
    in_specs = (
        P("mod", ("loop", "line"), None),
        P("mod", ("loop", "line"), None),
        P("mod", None, None),
        P("mod", "loop", "line"),
    )
    out_specs = (P("mod", "loop", None), P("mod", ("loop", "line"), None))
    return jax.shard_map(
        on_device, mesh=mesh, in_specs=in_specs, out_specs=out_specs, check_vma=False
    )
```

profile of v0, /device:TPU:8, one launch (start us, length us, event | category | flops | bytes accessed | tf_op | source)
XLA Modules:
  0.0 310.6 jit_solution(13326542029925265666)
XLA Ops:
  7.2 0.0 copy-start
  7.2 0.0 reduce-scatter.2.cloned.1.call-start
  8.0 0.7 copy-done
  8.7 3.9 %fusion.2 = f32[512,1280]{1,0:T(8,128)} fusion(bf16[1,768,1280]{2,1,0:T(8,128)(2,1)S(1)} %copy-done, bf16[1,768,512]{2,1,0:T(8,128)(2,1)} %param.4, pred[768]{0:T(1024)(128)(4,1)S(1)} %iota_compare_fusion), kind=kOutput, calls=%fused_computation.2 | convolution fusion | flops 1007026176 | bytes 5374720 | tf_op jit(solution)/shard_map/dot_general | solution.py:18
  12.7 0.0 copy-start.2
  12.7 0.0 reduce-scatter.2.cloned.1.call-update
  12.7 0.0 all-reduce.2.cloned.1.call-start
  12.8 101.7 %reduce-scatter.2.cloned.1.call-done = f32[32,1280]{1,0:T(8,128)} async-done(((f32[512,1280]{1,0:T(8,128)}), f32[32,1280]{1,0:T(8,128)}) %reduce-scatter.2.cloned.1.call-update) | async-done | bytes 163856 | tf_op jit(solution)/shard_map/reduce_scatter | solution.py:17
  114.5 0.0 all-reduce.2.cloned.1.call-update
  114.5 108.3 %all-reduce.2.cloned.1.call-done = f32[32,1280]{1,0:T(8,128)} async-done(((f32[32,1280]{1,0:T(8,128)}), f32[32,1280]{1,0:T(8,128)}) %all-reduce.2.cloned.1.call-update) | async-done | bytes 163856 | tf_op jit(solution)/shard_map/psum | solution.py:25
  222.8 1.6 multiply_reduce_fusion
  224.4 0.0 copy-done.2
  224.4 0.0 copy-start.1
  224.4 2.1 fusion.7
  226.5 75.9 %psum.15 = f32[]{:T(128)} all-reduce(f32[]{:T(128)} %multiply_reduce_fusion), channel_id=1, replica_groups=mesh['mod'=2,'loop'=16,'line'=16] {'mod','loop'}, use_global_device_ids=true, to_apply=%region_3.4 | all-reduce | flops 1 | bytes 8 | tf_op jit(solution)/shard_map/psum | solution.py:26
  303.1 0.0 copy-done.1
  303.1 0.7 multiply_bitcast_fusion
  (1 shorter events, 0.0 us)
Async XLA Ops:
  7.2 1.6 copy-start
  7.2 107.3 %reduce-scatter.2.cloned.1.call-start = ((), (), s32[]{:S(2)}) async-start(), calls=%async_computation.1 | async-start | bytes 2785280 | tf_op jit(solution)/shard_map/reduce_scatter | solution.py:17
  12.7 211.7 %copy-start.2 = (bf16[1,512,1280]{2,1,0:T(8,128)(2,1)S(1)}, bf16[1,512,1280]{2,1,0:T(8,128)(2,1)}, u32[]{:S(2)}) copy-start(bf16[1,512,1280]{2,1,0:T(8,128)(2,1)} %param.6) | copy-start | bytes 3932164
  12.7 210.1 %all-reduce.2.cloned.1.call-start = ((), (), s32[]{:S(2)}) async-start(), calls=%async_computation.2 | async-start | bytes 327680 | tf_op jit(solution)/shard_map/psum | solution.py:25
  224.4 78.7 %copy-start.1 = (f32[32,1280]{1,0:T(8,128)S(1)}, f32[32,1280]{1,0:T(8,128)}, u32[]{:S(2)}) copy-start(f32[32,1280]{1,0:T(8,128)} %all-reduce.2.cloned.1.call-done) | copy-start | bytes 491524
Sparse Core Ops, SparseCore 0:
  12.8 101.6 reduce-scatter.1
  116.8 105.9 all-reduce.1
where the time goes:
time: 311 us
  waiting for transfers between devices  210 us (68%)
  blocking collectives  75.9 us (24%)
  between operations  15.5 us (5%)
  matrix products  6.04 us (2%)
    psum x1, waiting for transfers between devices, on_device(): share = lax.psum(share, 'line')  108 us
    reduce_scatter x1, waiting for transfers between devices, on_device(): lax.psum_scatter(lax.dot_general(masked, upstream, (((0,), (0,)), ((), ()...  102 us
    psum x1, blocking collectives, on_device(): total = lax.psum(jnp.sum(share * share), ('mod', 'loop'))  75.9 us
  transfers between devices with their start and end apart: 2, of which 2 were waited for; matrix products, arithmetic and copies ran while one was open for 0% of the time, Pallas kernels for 0%

commit v1 on v0

--- a/solution.py
+++ b/solution.py
@@ -22,7 +22,7 @@
         scatter_dimension=0,
         tiled=True,
     )
-    share = lax.psum(share, "line")
+    share = jnp.sum(lax.all_gather(share, "line"), axis=0)
     total = lax.psum(jnp.sum(share * share), ("mod", "loop"))
     factor = 1.0 / jnp.sqrt(total / entries + 1e-06)
     clipped = share * factor

time: 311 us -> 246 us (0.79)
  waiting for transfers between devices: 210 us -> 143 us
    psum x1 -> x0, waiting for transfers between devices: 108 us -> none  [on_device(): share = lax.psum(share, 'line')]
    all_gather x0 -> x1, waiting for transfers between devices: none -> 41.7 us  [on_device(): share = jnp.sum(lax.all_gather(share, 'line'), axis=0)]
where the time goes in v1:
time: 246 us; the launch traced here: 245 us
  waiting for transfers between devices  143 us (58%)
  blocking collectives  76.3 us (31%)
  between operations  15.5 us (6%)
  matrix products  6.04 us (2%)
  other arithmetic  3.2 us (1%)
    reduce_scatter x1, waiting for transfers between devices, on_device(): lax.psum_scatter(lax.dot_general(masked, upstream, (((0,), (0,)), ((), ()...  102 us
    psum x1, blocking collectives, on_device(): total = lax.psum(jnp.sum(share * share), ('mod', 'loop'))  76.3 us
    all_gather x1, waiting for transfers between devices, on_device(): share = jnp.sum(lax.all_gather(share, 'line'), axis=0)  41.7 us
  transfers between devices with their start and end apart: 2, of which 2 were waited for; matrix products, arithmetic and copies ran while one was open for 0% of the time, Pallas kernels for 0%

profile of v1, /device:TPU:8, one launch (start us, length us, event | category | flops | bytes accessed | tf_op | source)
XLA Modules:
  0.0 245.4 jit_solution(3424943287230502218)
XLA Ops:
  7.2 0.0 copy-start
  7.2 0.0 reduce-scatter.2.cloned.1.call-start
  8.0 0.7 copy-done
  8.7 3.9 %fusion.2 = f32[512,1280]{1,0:T(8,128)} fusion(bf16[1,768,1280]{2,1,0:T(8,128)(2,1)S(1)} %copy-done, bf16[1,768,512]{2,1,0:T(8,128)(2,1)} %param.4, pred[768]{0:T(1024)(128)(4,1)S(1)} %iota_compare_fusion), kind=kOutput, calls=%fused_computation.2 | convolution fusion | flops 1007026176 | bytes 5374720 | tf_op jit(solution)/shard_map/dot_general | solution.py:18
  12.7 0.0 reduce-scatter.2.cloned.1.call-update
  12.7 0.0 copy-start.1
  12.7 0.0 all-gather.3.cloned.1.call-start
  12.8 101.7 %reduce-scatter.2.cloned.1.call-done = f32[32,1280]{1,0:T(8,128)} async-done(((f32[512,1280]{1,0:T(8,128)}), f32[32,1280]{1,0:T(8,128)}) %reduce-scatter.2.cloned.1.call-update) | async-done | bytes 163856 | tf_op jit(solution)/shard_map/reduce_scatter | solution.py:17
  114.5 0.0 all-gather.3.cloned.1.call-update
  114.5 41.7 %all-gather.3.cloned.1.call-done = f32[512,1280]{1,0:T(8,128)} async-done(((f32[32,1280]{1,0:T(8,128)}), f32[512,1280]{1,0:T(8,128)}) %all-gather.3.cloned.1.call-update) | async-done | bytes 2621456 | tf_op jit(solution)/shard_map/all_gather | solution.py:25
  156.3 1.9 reduce_sum.18
  158.1 0.6 multiply_reduce_fusion
  158.8 0.0 copy-done.1
  158.8 2.1 fusion.7
  160.9 76.3 %psum.7 = f32[]{:T(128)} all-reduce(f32[]{:T(128)} %multiply_reduce_fusion), channel_id=1, replica_groups=mesh['mod'=2,'loop'=16,'line'=16] {'mod','loop'}, use_global_device_ids=true, to_apply=%region_3.4 | all-reduce | flops 1 | bytes 8 | tf_op jit(solution)/shard_map/psum | solution.py:26
  237.8 0.7 multiply_bitcast_fusion
  (1 shorter events, 0.0 us)
Async XLA Ops:
  7.2 1.6 copy-start
  7.2 107.3 %reduce-scatter.2.cloned.1.call-start = ((), (), s32[]{:S(2)}) async-start(), calls=%async_computation.1 | async-start | bytes 2785280 | tf_op jit(solution)/shard_map/reduce_scatter | solution.py:17
  12.7 146.1 %copy-start.1 = (bf16[1,512,1280]{2,1,0:T(8,128)(2,1)S(1)}, bf16[1,512,1280]{2,1,0:T(8,128)(2,1)}, u32[]{:S(2)}) copy-start(bf16[1,512,1280]{2,1,0:T(8,128)(2,1)} %param.6) | copy-start | bytes 3932164
  12.7 143.5 %all-gather.3.cloned.1.call-start = ((), (), s32[]{:S(2)}) async-start(), calls=%async_computation.2 | async-start | bytes 2785280 | tf_op jit(solution)/shard_map/all_gather | solution.py:25
Sparse Core Ops, SparseCore 0:
  12.8 101.6 reduce-scatter.1
  116.6 39.5 all-gather.2
